TPU v7x, 512 devices: a whole 4x4x16 slice. The times are simulated.
512 devices in a mesh: sec: 4 (over z_hi), dev: 128 (over z_lo, y, x, core).
Axes of the slice: x: 4, y: 4, z: 16 (z_hi: 4, z_lo: 4; z = z_hi * 4 + z_lo), core: 2. Of those that a mesh axis runs over, the one named last changes fastest.
Arguments:
- queries: bfloat16 [256, 8192], P('dev', 'sec'), may hold values from -24 to 24
- cache_keys: bfloat16 [256, 4, 512, 128], P('dev', 'sec'), may hold values from -24 to 24
- cache_values: bfloat16 [256, 4, 512, 128], P('dev', 'sec'), may hold values from -48 to 48
- lengths: int32 [256], P('dev'), may hold values from 2 to 512, as said below
- out_proj: bfloat16 [4096, 8192], P('dev', 'sec'), may hold values from -0.0625 to 0.0625
- residual: bfloat16 [256, 4096], P(None, 'dev'), may hold values from -3 to 3
- norm_gain: bfloat16 [4096], replicated, may hold values from 0.5 to 1.5
- expert_ids: int32 [256, 8], replicated, may hold values from 0 to 127, all different within a row; in each aligned block of 256 rows (0 to 255, 256 to 511, ...) at most 48 rows name the same one
- gate_weights: float32 [256, 8], replicated, may hold values from 0.5 to 1.5
- owners: int32 [128], replicated, may hold values from 0 to 127, each once
- gate_proj: bfloat16 [128, 768, 4096], P('dev', 'sec'), may hold values from -0.09375 to 0.09375
- up_proj: bfloat16 [128, 768, 4096], P('dev', 'sec'), may hold values from -0.09375 to 0.09375
- down_proj: bfloat16 [128, 768, 4096], P('dev', 'sec'), may hold values from -0.21875 to 0.21875
Outputs:
- output: bfloat16 [256, 4096], P(None, 'dev')
Inputs may be any that keep to these rules, and one draw needn't show every extreme that they name: Row r's cache holds lengths[r] live positions from position 0; some row holds exactly 512. `expert_ids`: each row names 8 different experts; over all 256 rows no expert is named more than 48 times, a bound that some block reaches. Each index appears once; expert e's projections stand at index owners[e] of the expert projections.
All inputs are finite; a program needn't handle non-finite values.
Results may differ from a plain program's by a relative error of at most 0.009.
Values may be sent and summed in bfloat16 or wider, within the bound.
No kernel may reach another device: no remote copies, remote signals or barrier semaphores. Data moves between devices by JAX's collectives and lax.ppermute only.
A program may use at most 64 MiB of HBM per device.

v0:
```python
import math
import jax
import jax.numpy as jnp
from jax import lax
from jax.sharding import PartitionSpec as P

epsilon = 1e-05


def slot_targets(expert_ids, owners, capacity):
    experts = owners.shape[0]
    flat_ids = expert_ids.reshape(-1)
    one_hot = (flat_ids[:, None] == jnp.arange(experts, dtype=jnp.int32)[None, :]).astype(jnp.int32)
    before = jnp.cumsum(one_hot, axis=0) - one_hot
    position = jnp.sum(before * one_hot, axis=1)
    holder = jnp.sum(one_hot * owners[None, :], axis=1)
    return (holder * capacity + position).reshape(expert_ids.shape)


def routing_tables(expert_ids, gate_weights, owners, capacity):
    target = slot_targets(expert_ids, owners, capacity)
    places = jnp.arange(owners.shape[0] * capacity, dtype=jnp.int32)
    matched = target[None, :, :] == places[:, None, None]
    sending = jnp.any(matched, axis=2)
    weighting = jnp.sum(
        jnp.where(matched, gate_weights[None, :, :], jnp.zeros_like(gate_weights)[None, :, :]),
        axis=2,
    )
    return (sending, weighting)


def times_transpose(left, right):
    return lax.dot_general(
        left, right, (((1,), (1,)), ((), ())), preferred_element_type=jnp.float32
    )


def attend(queries, cache_keys, cache_values, lengths):
    rows, kv_heads, key_span, head_dim = cache_keys.shape
    group_size = queries.shape[1] // (kv_heads * head_dim)
    grouped = queries.reshape(rows, kv_heads, group_size, head_dim)
    scores = jnp.einsum(
        "rkgd,rktd->rkgt", grouped, cache_keys, preferred_element_type=jnp.float32
    ) / math.sqrt(head_dim)
    live_mask = (
        jnp.arange(key_span, dtype=jnp.int32)[None, None, None, :] < lengths[:, None, None, None]
    )
    scores = jnp.where(live_mask, scores, -jnp.inf)
    row_top = jnp.max(scores, axis=-1, keepdims=True)
    raised = jnp.exp(scores - row_top)
    soft_weight = (raised / jnp.sum(raised, axis=-1, keepdims=True)).astype(jnp.bfloat16)
    head_out = jnp.einsum(
        "rkgt,rktd->rkgd", soft_weight, cache_values, preferred_element_type=jnp.float32
    )
    return head_out.astype(jnp.bfloat16).reshape(rows, -1)


def root_norm(arrived, norm_gain):
    square_mean = jnp.mean(arrived * arrived, axis=-1, keepdims=True)
    return (arrived * lax.rsqrt(square_mean + epsilon) * norm_gain.astype(jnp.float32)).astype(
        jnp.bfloat16
    )


def expert_ffn(normed, gate_w, up_w, down_w):
    gate_act = times_transpose(normed, gate_w)
    up_act = times_transpose(normed, up_w)
    hidden = (jax.nn.silu(gate_act) * up_act).astype(jnp.bfloat16)
    return jnp.dot(hidden, down_w, preferred_element_type=jnp.float32)


def shards(
    queries,
    cache_keys,
    cache_values,
    lengths,
    out_proj,
    residual,
    norm_gain,
    expert_ids,
    gate_weights,
    owners,
    gate_proj,
    up_proj,
    down_proj,
):
    head_out = attend(queries, cache_keys, cache_values, lengths)
    attention_part = times_transpose(lax.all_gather(head_out, "dev", axis=0, tiled=True), out_proj)
    rows_all, top_count = expert_ids.shape
    experts = owners.shape[0]
    capacity = min(rows_all, 3 * top_count * rows_all // experts)
    col_count = out_proj.shape[0]
    sending, weighting = routing_tables(expert_ids, gate_weights, owners, capacity)
    residual_wide = residual.astype(jnp.float32)
    attention_out = lax.psum(attention_part, "sec")
    hidden_in = (residual_wide + attention_out).astype(jnp.bfloat16)
    outbound = jnp.dot(sending.astype(jnp.bfloat16), hidden_in, preferred_element_type=jnp.float32)
    outbound = outbound.astype(jnp.bfloat16).reshape(experts, capacity, col_count)
    inbound = lax.all_to_all(outbound, "dev", split_axis=0, concat_axis=2, tiled=True)
    arrived = inbound[0].astype(jnp.float32)
    normed = root_norm(arrived, norm_gain)
    expert_out = expert_ffn(normed, gate_proj[0], up_proj[0], down_proj[0])
    place_weight = jnp.sum(weighting, axis=1)
    own_weight = lax.dynamic_slice_in_dim(
        place_weight, lax.axis_index("dev") * capacity, capacity, 0
    )
    weighted = (expert_out * own_weight[:, None]).astype(jnp.bfloat16)
    returned = lax.all_to_all(
        weighted.reshape(1, capacity, weighted.shape[1]),
        "dev",
        split_axis=2,
        concat_axis=0,
        tiled=True,
    )
    moe = jnp.dot(
        sending.T.astype(jnp.bfloat16),
        returned.reshape(-1, col_count),
        preferred_element_type=jnp.float32,
    )
    summed = lax.psum(moe, "sec")
    return (residual_wide + attention_out + summed).astype(jnp.bfloat16)


def solution(mesh):
    in_specs = (
        P("dev", "sec"),
        P("dev", "sec", None, None),
        P("dev", "sec", None, None),
        P("dev"),
        P("dev", "sec"),
        P(None, "dev"),
        P(),
        P(),
        P(),
        P(),
        P("dev", "sec", None),
        P("dev", "sec", None),
        P("dev", "sec", None),
    )
    out_specs = P(None, "dev")
    return jax.shard_map(shards, mesh=mesh, in_specs=in_specs, out_specs=out_specs, check_vma=False)
```

profile of v0, /device:TPU:8, one launch (start us, length us, event | category | flops | bytes accessed | tf_op | source)
XLA Modules:
  0.0 469.7 jit_solution(8240193825732816085)
XLA Ops:
  6.5 0.0 copy-start
  6.5 0.0 all-gather.3.cloned.1.call-start
  6.5 0.8 iota_compare_fusion.4
  7.4 1.1 fusion.14
  8.5 0.2 fusion.43
  8.7 1.2 convolution_convert_fusion.1
  9.9 0.6 reshape.152
  10.5 0.0 all-gather.3.cloned.1.call-update
  10.5 0.8 copy.33
  11.4 0.1 eq.42
  11.5 0.1 eq.38
  11.6 0.1 copy.35
  11.7 0.3 fusion.23
  12.1 0.1 broadcast_add_fusion
  12.2 0.0 copy-start.9
  12.2 0.3 copy.36
  12.5 0.3 copy-done.9
  12.8 1.1 select_reduce_fusion.1
  13.9 0.1 add.41
  14.0 0.1 copy.37
  14.1 57.2 %fusion.1 = pred[6144,256]{1,0:T(8,128)(4,1)} fusion(s32[256,8]{0,1:T(8,128)S(1)} %copy.37), kind=kLoop, calls=%fused_computation.3 | loop fusion | flops 23592960 | bytes 1581056 | tf_op jit(solution)/shard_map/reduce_or | solution.py:24
  71.3 146.4 %all-gather.3.cloned.1.call-done = bf16[128,2,2048]{2,1,0:T(2,128)(2,1)} async-done(((bf16[1,2,2048]{2,1,0:T(2,128)(2,1)}), bf16[128,2,2048]{2,1,0:T(2,128)(2,1)}) %all-gather.3.cloned.1.call-update) | async-done | bytes 1048592 | tf_op jit(solution)/shard_map/all_gather | solution.py:88
  217.7 1.5 reshape.153
  219.2 0.0 copy-done.4
  219.2 0.4 fusion.44
  219.6 25.8 %psum.14 = f32[256,32]{0,1:T(8,128)S(1)} all-reduce(f32[256,32]{0,1:T(8,128)S(1)} %fusion.44), channel_id=1, replica_groups=mesh['sec'=4,'dev'=128] {'sec'}, use_global_device_ids=true, to_apply=%region_2.3 | all-reduce | flops 8192 | bytes 65536 | tf_op jit(solution)/shard_map/psum | solution.py:95
  245.5 0.0 copy-start.5
  245.5 0.6 copy-done.5
  246.1 0.0 copy-done.7
  246.1 2.4 convolution_convert_fusion
  248.5 1.1 reshape.147
  249.6 1.7 copy.50
  251.3 3.4 reshape.155
  254.7 9.2 %all-to-all-start = ((bf16[128,2,768]{2,1,0:T(2,128)(2,1)}), bf16[128,2,768]{2,1,0:T(2,128)(2,1)S(1)}, u32[]{:S(2)}, u32[]{:S(2)}) async-start(bf16[128,2,768]{2,1,0:T(2,128)(2,1)} %reshape.155), calls=%async_computation | async-start | bytes 786432 | tf_op jit(solution)/shard_map/all_to_all | solution.py:99
  263.9 0.0 copy-done.8
  263.9 0.1 reshape.151
  264.0 0.0 copy-done.10
  264.0 91.4 %select_reduce_fusion = f32[6144]{0:T(1024)S(1)} fusion(f32[256,8]{0,1:T(8,128)S(1)} %copy-done.10, s32[256,8]{0,1:T(8,128)S(1)} %copy.37), kind=kLoop, calls=%fused_computation.1 | loop fusion | flops 37742592 | bytes 40960 | tf_op jit(solution)/shard_map/reduce_sum | solution.py:103
  355.4 0.6 dynamic_slice.3
  355.9 0.0 all-to-all-done
  356.0 1.0 reshape.156
  357.0 0.0 copy-start.2
  357.0 0.6 fusion.4
  357.6 0.7 fusion.6
  358.3 0.0 copy-start.1
  358.3 0.0 copy-start.3
  358.3 1.0 copy-done.1
  359.3 0.0 copy-done.2
  359.3 1.2 fusion.10
  360.4 0.0 copy-done
  360.4 2.5 fusion.3
  362.9 3.9 copy.40
  366.8 0.5 broadcast.89
  367.3 23.6 %reduce.7 = bf16[4096,48]{1,0:T(8,128)(2,1)S(1)} reduce(bf16[4096,1,48]{2,1,0:T(2,128)(2,1)} %bitcast.71, bf16[]{:T(256)} %broadcast.89), dimensions={1}, to_apply=%bitcast.53.reduce_sub_computation | reduce | bytes 786434
  390.9 1.4 reshape.157
  392.3 27.2 %all_to_all.24 = bf16[128,2,768]{2,1,0:T(2,128)(2,1)S(1)} all-to-all(bf16[128,2,768]{2,1,0:T(2,128)(2,1)S(1)} %reshape.157), channel_id=1, replica_groups=mesh['sec'=4,'dev'=128] {'dev'}, dimensions={0} | all-to-all | bytes 786432 | tf_op jit(solution)/shard_map/all_to_all | solution.py:108
  419.5 4.1 reshape.158
  423.6 4.6 copy.41
  428.1 1.3 all_to_all.20
  429.4 3.4 copy.42
  432.8 2.8 reshape.149
  435.6 2.3 fusion.45
  437.9 24.1 %psum.15 = f32[256,32]{0,1:T(8,128)S(1)} all-reduce(f32[256,32]{0,1:T(8,128)S(1)} %fusion.45), channel_id=1, replica_groups=mesh['sec'=4,'dev'=128] {'sec'}, use_global_device_ids=true, to_apply=%region_10.11 | all-reduce | flops 8192 | bytes 65536 | tf_op jit(solution)/shard_map/psum | solution.py:120
  462.0 0.6 add_convert_fusion
  (12 shorter events, 0.1 us)
Async XLA Ops:
  6.5 353.9 %copy-start = (bf16[1,192,4096]{2,1,0:T(8,128)(2,1)S(1)}, bf16[1,192,4096]{2,1,0:T(8,128)(2,1)}, u32[]{:S(2)}) copy-start(bf16[1,192,4096]{2,1,0:T(8,128)(2,1)} %param.25) | copy-start | bytes 4718596
  6.5 211.2 %all-gather.3.cloned.1.call-start = ((), (), s32[]{:S(2)}) async-start(), calls=%async_computation.2 | async-start | bytes 1056768 | tf_op jit(solution)/shard_map/all_gather | solution.py:88
  12.2 0.7 copy-start.9
  14.1 205.1 %copy-start.4 = (bf16[32,2048]{1,0:T(8,128)(2,1)S(1)}, bf16[32,2048]{1,0:T(8,128)(2,1)}, u32[]{:S(2)}) copy-start(bf16[32,2048]{1,0:T(8,128)(2,1)} %param.17) | copy-start | bytes 393220
  71.3 174.8 %copy-start.7 = (bf16[256,32]{0,1:T(8,128)(2,1)S(1)}, bf16[256,32]{0,1:T(8,128)(2,1)}, u32[]{:S(2)}) copy-start(bf16[256,32]{0,1:T(8,128)(2,1)} %param.18) | copy-start | bytes 49156
  245.5 0.6 copy-start.5
  251.3 12.6 %copy-start.8 = (bf16[4096]{0:T(1024)(128)(2,1)S(1)}, bf16[4096]{0:T(1024)(128)(2,1)}, u32[]{:S(2)}) copy-start(bf16[4096]{0:T(1024)(128)(2,1)} %param.19) | copy-start | bytes 24580
  251.3 12.7 %copy-start.10 = (f32[256,8]{0,1:T(8,128)S(1)}, f32[256,8]{0,1:T(8,128)}, u32[]{:S(2)}) copy-start(f32[256,8]{0,1:T(8,128)} %param.21) | copy-start | bytes 24580
  254.7 101.3 %all-to-all-start = ((bf16[128,2,768]{2,1,0:T(2,128)(2,1)}), bf16[128,2,768]{2,1,0:T(2,128)(2,1)S(1)}, u32[]{:S(2)}, u32[]{:S(2)}) async-start(bf16[128,2,768]{2,1,0:T(2,128)(2,1)} %reshape.155), calls=%async_computation | async-start | bytes 786432 | tf_op jit(solution)/shard_map/all_to_all | solution.py:99
  357.0 2.3 copy-start.2
  358.3 1.0 copy-start.1
  358.3 2.2 copy-start.3
  435.5 26.4 %copy-start.6 = (f32[256,32]{0,1:T(8,128)S(1)}, f32[256,32]{0,1:T(8,128)}, u32[]{:S(2)}) copy-start(f32[256,32]{0,1:T(8,128)} %copy-done.5) | copy-start | bytes 98308
Sparse Core Ops, SparseCore 0:
  10.7 207.0 all-gather.2
where the time goes:
time: 476 us; the launch traced here: 470 us
  other arithmetic  177 us (37%)
  waiting for transfers between devices  146 us (31%)
  blocking collectives  77.1 us (16%)
  local copies, waits for them, and re-layouts  35.3 us (7%)
  between operations  13.9 us (3%)
  matrix products  11.1 us (2%)
  starting transfers between devices  9.19 us (2%)
    all_gather x1, waiting for transfers between devices, shards(): lax.all_gather(head_out, 'dev', axis=0, tiled=True)  146 us
    reduce_sum x1, other arithmetic, shards(): place_weight = jnp.sum(weighting, axis=1)  91.4 us
    reduce_or x1, other arithmetic, routing_tables(): sending = jnp.any(matched, axis=2)  57.2 us
    all_to_all x1, blocking collectives, shards(): lax.all_to_all(weighted.reshape(1, capacity, weighted.shape[1]), 'dev', s...  27.2 us
    psum x1, blocking collectives, shards(): attention_out = lax.psum(attention_part, 'sec')  25.8 us
    psum x1, blocking collectives, shards(): summed = lax.psum(moe, 'sec')  24.1 us
    unnamed x1, other arithmetic  23.6 us
    unnamed x30, local copies, waits for them, and re-layouts  15.2 us
  transfers between devices with their start and end apart: 2, of which 1 were waited for; matrix products, arithmetic and copies ran while one was open for 32% of the time, Pallas kernels for 0%

commit v1 on v0

--- a/solution.py
+++ b/solution.py
@@ -105,12 +105,18 @@
         place_weight, lax.axis_index("dev") * capacity, capacity, 0
     )
     weighted = (expert_out * own_weight[:, None]).astype(jnp.bfloat16)
-    returned = lax.all_to_all(
-        weighted.reshape(1, capacity, weighted.shape[1]),
-        "dev",
-        split_axis=2,
-        concat_axis=0,
-        tiled=True,
+    returned = jnp.concatenate(
+        lax.all_to_all(
+            jnp.stack(
+                jnp.split(
+                    weighted.reshape(1, capacity, weighted.shape[1]), lax.axis_size("dev"), axis=2
+                )
+            ),
+            "dev",
+            0,
+            0,
+        ),
+        axis=0,
     )
     moe = jnp.dot(
         sending.T.astype(jnp.bfloat16),

time: 476 us -> 516 us (1.084); the launches traced: 470 us -> 515 us
  local copies, waits for them, and re-layouts: 35.3 us -> 106 us
  other arithmetic: 177 us -> 153 us
    unnamed x30 -> x156, local copies, waits for them, and re-layouts: 15.2 us -> 94.9 us
    unnamed x1 -> x0, other arithmetic: 23.6 us -> none
    all_to_all x3 -> x1, local copies, waits for them, and re-layouts: 9.21 us -> 1.37 us  [shards(): lax.all_to_all(jnp.stack(jnp.split(weighted.reshape(1, capacity, weighted...]
    reshape x2 -> x0, local copies, waits for them, and re-layouts: 6.62 us -> none  [the longest x1 3.86 us: shards(): weighted.reshape(1, capacity, weighted.shape[1])]
    another operation x3 -> x6, local copies, waits for them, and re-layouts: 0.35 us -> 5.84 us  [the longest x1 2.77 us: shards(): returned.reshape(-1, col_count)]
  transfers between devices with their start and end apart: 2 -> 2, of which waited for: 1 -> 1; matrix products, arithmetic and copies ran while one was open for 32% -> 30% of each run, Pallas kernels for 0% -> 0%
where the time goes in v1:
time: 516 us; the launch traced here: 515 us
  other arithmetic  153 us (30%)
  waiting for transfers between devices  146 us (28%)
  local copies, waits for them, and re-layouts  106 us (21%)
  blocking collectives  76.5 us (15%)
  between operations  13.7 us (3%)
  matrix products  11.1 us (2%)
  starting transfers between devices  8.56 us (2%)
    all_gather x1, waiting for transfers between devices, shards(): lax.all_gather(head_out, 'dev', axis=0, tiled=True)  146 us
    unnamed x156, local copies, waits for them, and re-layouts  94.9 us
    reduce_sum x1, other arithmetic, shards(): place_weight = jnp.sum(weighting, axis=1)  91.4 us
    reduce_or x1, other arithmetic, routing_tables(): sending = jnp.any(matched, axis=2)  57.2 us
    all_to_all x1, blocking collectives, shards(): lax.all_to_all(jnp.stack(jnp.split(weighted.reshape(1, capacity, weighted...  27 us
    psum x1, blocking collectives, shards(): attention_out = lax.psum(attention_part, 'sec')  25.4 us
    psum x1, blocking collectives, shards(): summed = lax.psum(moe, 'sec')  24.1 us
  transfers between devices with their start and end apart: 2, of which 1 were waited for; matrix products, arithmetic and copies ran while one was open for 30% of the time, Pallas kernels for 0%

profile of v1, /device:TPU:8, one launch (start us, length us, event | category | flops | bytes accessed | tf_op | source)
XLA Modules:
  0.0 515.3 jit_solution(7048621202383778954)
XLA Ops:
  6.5 0.8 iota_compare_fusion.4
  7.4 1.1 fusion.14
  8.7 1.2 convolution_convert_fusion.1
  10.5 0.8 copy.295
  12.8 1.1 select_reduce_fusion.1
  14.1 57.2 %fusion.1 = pred[6144,256]{1,0:T(8,128)(4,1)} fusion(s32[256,8]{0,1:T(8,128)S(1)} %copy.299), kind=kLoop, calls=%fused_computation.3 | loop fusion | flops 23592960 | bytes 1581056 | tf_op jit(solution)/shard_map/reduce_or | solution.py:24
  71.3 146.4 %all-gather.3.cloned.1.call-done = bf16[128,2,2048]{2,1,0:T(2,128)(2,1)} async-done(((bf16[1,2,2048]{2,1,0:T(2,128)(2,1)}), bf16[128,2,2048]{2,1,0:T(2,128)(2,1)}) %all-gather.3.cloned.1.call-update) | async-done | bytes 1048592 | tf_op jit(solution)/shard_map/all_gather | solution.py:88
  217.7 1.5 reshape.148
  219.6 25.4 %psum.14 = f32[256,32]{0,1:T(8,128)S(1)} all-reduce(f32[256,32]{0,1:T(8,128)S(1)} %fusion.44), channel_id=1, replica_groups=mesh['sec'=4,'dev'=128] {'sec'}, use_global_device_ids=true, to_apply=%region_2.3 | all-reduce | flops 8192 | bytes 65536 | tf_op jit(solution)/shard_map/psum | solution.py:95
  245.7 2.4 convolution_convert_fusion
  248.1 1.1 reshape.143
  249.2 1.6 copy.311
  250.9 3.4 reshape.150
  254.3 8.6 %all-to-all-start = ((bf16[128,2,768]{2,1,0:T(2,128)(2,1)}), bf16[128,2,768]{2,1,0:T(2,128)(2,1)S(1)}, u32[]{:S(2)}, u32[]{:S(2)}) async-start(bf16[128,2,768]{2,1,0:T(2,128)(2,1)} %reshape.150), calls=%async_computation | async-start | bytes 786432 | tf_op jit(solution)/shard_map/all_to_all | solution.py:99
  262.9 91.4 %select_reduce_fusion = f32[6144]{0:T(1024)S(1)} fusion(f32[256,8]{0,1:T(8,128)S(1)} %copy-done.10, s32[256,8]{0,1:T(8,128)S(1)} %copy.299), kind=kLoop, calls=%fused_computation.1 | loop fusion | flops 37742592 | bytes 40960 | tf_op jit(solution)/shard_map/reduce_sum | solution.py:103
  354.9 1.0 reshape.151
  356.5 0.7 fusion.6
  357.3 0.9 copy-done.1
  358.2 1.2 fusion.10
  359.4 2.5 fusion.3
  362.5 0.7 constant_dynamic-update-slice_fusion.126
  365.8 0.7 constant_dynamic-update-slice_fusion.121
  373.0 0.7 constant_dynamic-update-slice_fusion.110
  373.6 0.7 constant_dynamic-update-slice_fusion.109
  378.2 0.7 constant_dynamic-update-slice_fusion.102
  378.9 0.7 constant_dynamic-update-slice_fusion.101
  381.5 0.7 constant_dynamic-update-slice_fusion.97
  382.2 0.7 constant_dynamic-update-slice_fusion.96
  387.4 0.7 constant_dynamic-update-slice_fusion.88
  389.4 0.7 constant_dynamic-update-slice_fusion.85
  391.3 0.7 constant_dynamic-update-slice_fusion.82
  392.7 0.7 constant_dynamic-update-slice_fusion.80
  394.6 0.7 constant_dynamic-update-slice_fusion.77
  397.3 0.7 constant_dynamic-update-slice_fusion.73
  399.2 0.7 constant_dynamic-update-slice_fusion.70
  399.9 0.7 constant_dynamic-update-slice_fusion.69
  400.6 0.7 constant_dynamic-update-slice_fusion.68
  402.5 0.7 constant_dynamic-update-slice_fusion.65
  405.1 0.7 constant_dynamic-update-slice_fusion.61
  407.8 0.7 constant_dynamic-update-slice_fusion.57
  409.7 0.7 constant_dynamic-update-slice_fusion.54
  410.4 0.7 constant_dynamic-update-slice_fusion.53
  416.3 0.7 constant_dynamic-update-slice_fusion.44
  418.3 0.7 constant_dynamic-update-slice_fusion.41
  420.2 0.7 constant_dynamic-update-slice_fusion.38
  422.8 0.7 constant_dynamic-update-slice_fusion.34
  424.2 0.7 constant_dynamic-update-slice_fusion.32
  426.8 0.7 constant_dynamic-update-slice_fusion.28
  428.1 0.7 constant_dynamic-update-slice_fusion.26
  429.4 0.7 constant_dynamic-update-slice_fusion.24
  431.4 0.7 constant_dynamic-update-slice_fusion.21
  432.1 0.7 constant_dynamic-update-slice_fusion.20
  434.0 0.7 constant_dynamic-update-slice_fusion.17
  437.3 0.7 constant_dynamic-update-slice_fusion.12
  441.2 0.7 constant_dynamic-update-slice_fusion.6
  441.9 0.7 constant_dynamic-update-slice_fusion.5
  445.8 2.1 copy.302
  447.9 1.4 reshape.152
  449.3 27.0 %all_to_all.14 = bf16[128,2,768]{2,1,0:T(2,128)(2,1)S(1)} all-to-all(bf16[128,2,768]{2,1,0:T(2,128)(2,1)S(1)} %reshape.152), channel_id=1, replica_groups=mesh['sec'=4,'dev'=128] {'dev'}, dimensions={0} | all-to-all | bytes 786432 | tf_op jit(solution)/shard_map/all_to_all | solution.py:109
  476.3 1.0 reshape.153
  477.3 1.4 copy.303
  478.7 2.8 reshape_reshape.3
  481.5 2.3 fusion.45
  483.8 24.1 %psum.15 = f32[256,32]{0,1:T(8,128)S(1)} all-reduce(f32[256,32]{0,1:T(8,128)S(1)} %fusion.45), channel_id=1, replica_groups=mesh['sec'=4,'dev'=128] {'sec'}, use_global_device_ids=true, to_apply=%region_10.11 | all-reduce | flops 8192 | bytes 65536 | tf_op jit(solution)/shard_map/psum | solution.py:126
  (136 shorter events, 64.8 us)
Async XLA Ops:
  6.5 352.8 %copy-start = (bf16[1,192,4096]{2,1,0:T(8,128)(2,1)S(1)}, bf16[1,192,4096]{2,1,0:T(8,128)(2,1)}, u32[]{:S(2)}) copy-start(bf16[1,192,4096]{2,1,0:T(8,128)(2,1)} %param.25) | copy-start | bytes 4718596
  6.5 211.2 %all-gather.3.cloned.1.call-start = ((), (), s32[]{:S(2)}) async-start(), calls=%async_computation.2 | async-start | bytes 1056768 | tf_op jit(solution)/shard_map/all_gather | solution.py:88
  12.2 0.7 copy-start.9
  14.1 205.1 %copy-start.4 = (bf16[32,2048]{1,0:T(8,128)(2,1)S(1)}, bf16[32,2048]{1,0:T(8,128)(2,1)}, u32[]{:S(2)}) copy-start(bf16[32,2048]{1,0:T(8,128)(2,1)} %param.17) | copy-start | bytes 393220
  71.3 174.4 %copy-start.7 = (bf16[256,32]{0,1:T(8,128)(2,1)S(1)}, bf16[256,32]{0,1:T(8,128)(2,1)}, u32[]{:S(2)}) copy-start(bf16[256,32]{0,1:T(8,128)(2,1)} %param.18) | copy-start | bytes 49156
  245.1 0.6 copy-start.5
  250.9 12.0 %copy-start.8 = (bf16[4096]{0:T(1024)(128)(2,1)S(1)}, bf16[4096]{0:T(1024)(128)(2,1)}, u32[]{:S(2)}) copy-start(bf16[4096]{0:T(1024)(128)(2,1)} %param.19) | copy-start | bytes 24580
  250.9 12.1 %copy-start.10 = (f32[256,8]{0,1:T(8,128)S(1)}, f32[256,8]{0,1:T(8,128)}, u32[]{:S(2)}) copy-start(f32[256,8]{0,1:T(8,128)} %param.21) | copy-start | bytes 24580
  254.3 100.6 %all-to-all-start = ((bf16[128,2,768]{2,1,0:T(2,128)(2,1)}), bf16[128,2,768]{2,1,0:T(2,128)(2,1)S(1)}, u32[]{:S(2)}, u32[]{:S(2)}) async-start(bf16[128,2,768]{2,1,0:T(2,128)(2,1)} %reshape.150), calls=%async_computation | async-start | bytes 786432 | tf_op jit(solution)/shard_map/all_to_all | solution.py:99
  356.0 2.3 copy-start.2
  357.2 1.0 copy-start.1
  357.3 2.1 copy-start.3
  481.4 26.4 %copy-start.6 = (f32[256,32]{0,1:T(8,128)S(1)}, f32[256,32]{0,1:T(8,128)}, u32[]{:S(2)}) copy-start(f32[256,32]{0,1:T(8,128)} %copy-done.5) | copy-start | bytes 98308
Sparse Core Ops, SparseCore 0:
  10.7 207.0 all-gather.2
